TPU v7x, 32 devices: a whole 2x2x4 slice. The times are simulated.
32 devices in a mesh: groups: 2 (over y), shard: 4 (over z), pair: 4 (over x, core).
Axes of the slice: x: 2, y: 2, z: 4, core: 2. Of those that a mesh axis runs over, the one named last changes fastest.
Arguments:
- gradient: bfloat16 [2, 8, 512, 512], P('groups', None, 'shard'), parts along dimension 0, may hold values from -6.5 to 6.5, as said below
- momentum: bfloat16 [2, 8, 512, 512], P('groups', None, 'shard'), parts along dimension 0, may hold values from -6.5 to 6.5, as said below
Outputs:
- update: bfloat16 [2, 8, 512, 512], P('groups', None, 'shard'), parts along dimension 0
- new_momentum: bfloat16 [2, 8, 512, 512], P('groups', None, 'shard'), parts along dimension 0
There are 2 independent parts, one for each index of `groups`. A program takes and returns all parts, laid end to end along the dimension named above; each array names one. Nothing has to cross between parts.
Inputs may be any that keep to these rules, and one draw needn't show every extreme that they name: `gradient`: entries of order one. `momentum`: entries of order one.
All inputs are finite; a program needn't handle non-finite values.
Results may differ from a plain program's by a relative error of at most 0.0053.
Values may be sent and summed in bfloat16 or wider, within the bound.
A program may use at most 64 MiB of HBM per device.

v0:
```python
import jax
import jax.numpy as jnp
from jax import lax
from jax.sharding import PartitionSpec as P

damping = 0.1
decay_rate = 0.9


def from_partner(value, axis, apart):
    mask = 2**apart
    pairs = [(source, source ^ mask) for source in range(lax.axis_size(axis))]
    return lax.ppermute(value, axis, pairs)


def multiply(left_matrix, right_matrix):
    return jnp.dot(
        left_matrix,
        right_matrix,
        precision=lax.Precision.HIGHEST,
        preferred_element_type=jnp.float32,
    )


def gram_root(gram_matrix):
    block_size = gram_matrix.shape[0]
    identity = jnp.eye(block_size, dtype=jnp.float32)
    scaling = 2.0 * jnp.trace(gram_matrix) / block_size
    root_scale = jnp.sqrt(jnp.sqrt(scaling))
    scaled = gram_matrix / scaling
    leading = (5.0 * identity - scaled) / 4.0
    iterate = leading / root_scale
    squared = multiply(leading, leading)
    fourth = multiply(squared, squared)
    shifted = multiply(fourth, scaled)
    second = (5.0 * identity - shifted) / 4.0
    return multiply(iterate, second)


def local(gradient, momentum):
    new_momentum = (
        decay_rate * momentum.astype(jnp.float32) + gradient.astype(jnp.float32)
    ).astype(jnp.bfloat16)
    block_rows, block_cols, local_rows, block_size = gradient.shape
    half_cols = block_cols // 2
    half_width = block_size // 2
    shards = lax.axis_size("shard")
    position = lax.axis_index("pair")
    column_half = position // 2
    side_index = position % 2
    leading_side = side_index == 0
    grad_half = lax.dynamic_slice_in_dim(gradient, column_half * half_cols, half_cols, 1).reshape(
        shards, local_rows, block_size
    )
    mom_half = lax.dynamic_slice_in_dim(
        new_momentum, column_half * half_cols, half_cols, 1
    ).reshape(shards, local_rows, block_size)
    grad_recv, mom_recv = (
        lax.all_to_all(grad_half, "shard", split_axis=0, concat_axis=1, tiled=True),
        lax.all_to_all(mom_half, "shard", split_axis=0, concat_axis=1, tiled=True),
    )
    grad_block = grad_recv[0]
    mom_block = mom_recv[0]
    identity = jnp.eye(block_size, dtype=jnp.float32)
    oriented = jnp.where(leading_side, grad_block, grad_block.T)
    gram_matrix = (
        jnp.dot(oriented, oriented.T, preferred_element_type=jnp.float32) / block_size
        + damping * identity
    )
    own_root = gram_root(gram_matrix)
    partner = from_partner(own_root, "pair", 0)
    left_root = jnp.where(leading_side, own_root, partner)
    right_root = jnp.where(leading_side, partner, own_root)
    right_part = lax.dynamic_slice_in_dim(right_root, side_index * half_width, half_width, 1)
    partial_prod = multiply(mom_block.astype(jnp.float32), right_part)
    own_piece = multiply(left_root, partial_prod).astype(jnp.bfloat16)
    outgoing = own_piece.reshape(shards, local_rows, half_width)
    returned = lax.all_to_all(outgoing, "shard", split_axis=0, concat_axis=0, tiled=True)
    own_rows = returned.reshape(block_rows, half_cols, local_rows, half_width)
    gathered = lax.all_gather(own_rows[None], "pair", axis=0, tiled=True)
    update = (
        gathered.reshape(2, 2, block_rows, half_cols, local_rows, half_width)
        .transpose(2, 0, 3, 4, 1, 5)
        .reshape(block_rows, block_cols, local_rows, block_size)
    )
    return (update, new_momentum)


def solution(mesh):
    in_specs = (P("groups", None, "shard", None), P("groups", None, "shard", None))
    out_specs = (P("groups", None, "shard", None), P("groups", None, "shard", None))
    return jax.shard_map(local, mesh=mesh, in_specs=in_specs, out_specs=out_specs, check_vma=False)
```

profile of v0, /device:TPU:0, one launch (start us, length us, event | category | flops | bytes accessed | tf_op | source)
XLA Modules:
  0.0 102.2 jit_solution(1875327581618212463)
XLA Ops:
  7.2 1.9 %dynamic-slice_bitcast_fusion.1 = bf16[4,128,512]{2,1,0:T(8,128)(2,1)} fusion(bf16[1,8,128,512]{3,2,1,0:T(8,128)(2,1)} %param.2, s32[]{:T(128)S(6)} %select_n.44), kind=kLoop, calls=%fused_computation.23 | loop fusion | bytes 1048580 | tf_op jit(solution)/shard_map/reshape | solution.py:52
  9.1 6.3 %all-to-all-start = ((bf16[4,128,512]{2,1,0:T(8,128)(2,1)}), bf16[4,128,512]{2,1,0:T(8,128)(2,1)S(1)}, u32[]{:S(2)}, u32[]{:S(2)}) async-start(bf16[4,128,512]{2,1,0:T(8,128)(2,1)} %dynamic-slice_bitcast_fusion.1), calls=%async_computation | async-start | bytes 1048576 | tf_op jit(solution)/shard_map/all_to_all | solution.py:59
  15.4 14.5 %all-to-all-done = bf16[4,128,512]{2,1,0:T(8,128)(2,1)S(1)} async-done(((bf16[4,128,512]{2,1,0:T(8,128)(2,1)}), bf16[4,128,512]{2,1,0:T(8,128)(2,1)S(1)}, u32[]{:S(2)}, u32[]{:S(2)}) %all-to-all-start) | async-done | bytes 524320 | tf_op jit(solution)/shard_map/all_to_all | solution.py:59
  29.9 0.2 copy.12
  30.1 1.1 %select_reduce_fusion = (f32[]{:T(128)}, f32[512,512]{1,0:T(8,128)S(1)}) fusion(bf16[512,512]{1,0:T(8,128)(2,1)S(1)} %bitcast.22, bf16[512,512]{0,1:T(8,128)(2,1)S(1)} %copy.12, pred[]{:T(512)S(6)} %eq.17), kind=kOutput, calls=%fused_computation.11 | convolution fusion | flops 270270464 | bytes 2097157 | tf_op jit(solution)/shard_map/dot_general | solution.py:67
  31.9 2.0 %fusion.6 = f32[512,512]{1,0:T(8,128)S(1)} fusion(f32[512,512]{1,0:T(8,128)S(1)} %get-tuple-element.3, f32[]{:T(128)S(6)} %div.40), kind=kOutput, calls=%fused_computation.13 | convolution fusion | flops 1611923456 | bytes 2097156 | tf_op jit(solution)/shard_map/dot_general | solution.py:17
  33.9 1.8 %fusion.28 = f32[512,512]{1,0:T(8,128)S(1)} fusion(f32[512,512]{1,0:T(8,128)S(1)} %fusion.6), kind=kOutput, calls=%fused_computation.38 | convolution fusion | flops 1610612736 | bytes 2097152 | tf_op jit(solution)/shard_map/dot_general | solution.py:17
  35.7 1.9 %fusion.1 = f32[512,512]{1,0:T(8,128)S(1)} fusion(f32[512,512]{1,0:T(8,128)S(1)} %fusion.28, f32[512,512]{1,0:T(8,128)S(1)} %get-tuple-element.3, f32[]{:T(128)S(6)} %div.40), kind=kOutput, calls=%fused_computation.5 | convolution fusion | flops 1611923456 | bytes 3145732 | tf_op jit(solution)/shard_map/dot_general | solution.py:17
  37.6 0.0 copy-start
  37.7 2.0 %fusion.4 = f32[512,512]{1,0:T(8,128)S(1)} fusion(f32[512,512]{1,0:T(8,128)S(1)} %fusion.1, f32[]{:T(128)S(6)} %sqrt.7, f32[512,512]{1,0:T(8,128)S(1)} %get-tuple-element.3, f32[]{:T(128)S(6)} %div.40), kind=kOutput, calls=%fused_computation.9 | convolution fusion | flops 1612185600 | bytes 3145736 | tf_op jit(solution)/shard_map/dot_general | solution.py:17
  39.7 0.1 collective-permute-start
  39.8 0.4 add_convert_fusion
  40.1 0.9 dynamic-slice_bitcast_fusion
  41.0 0.2 copy-done.1
  41.3 4.1 %all-to-all-start.1 = ((bf16[4,128,512]{2,1,0:T(8,128)(2,1)}), bf16[4,128,512]{2,1,0:T(8,128)(2,1)}, u32[]{:S(2)}, u32[]{:S(2)}) async-start(bf16[4,128,512]{2,1,0:T(8,128)(2,1)} %dynamic-slice_bitcast_fusion), calls=%async_computation.1 | async-start | bytes 1048576 | tf_op jit(solution)/shard_map/all_to_all | solution.py:60
  45.4 0.0 all-gather.3.cloned.1.call-start
  45.5 15.4 %all-to-all-done.1 = bf16[4,128,512]{2,1,0:T(8,128)(2,1)} async-done(((bf16[4,128,512]{2,1,0:T(8,128)(2,1)}), bf16[4,128,512]{2,1,0:T(8,128)(2,1)}, u32[]{:S(2)}, u32[]{:S(2)}) %all-to-all-start.1) | async-done | bytes 524320 | tf_op jit(solution)/shard_map/all_to_all | solution.py:60
  60.9 1.7 %fusion.9 = f32[512,256]{1,0:T(8,128)S(1)} fusion(bf16[512,512]{1,0:T(8,128)(2,1)} %bitcast.4, f32[512,512]{1,0:T(8,128)S(1)} %fusion.4, s32[]{:T(128)S(6)} %select_n.49, f32[512,512]{1,0:T(8,128)S(1)} %collective-permute-done, pred[]{:T(512)S(6)} %eq.17), kind=kOutput, calls=%fused_computation.15 | convolution fusion | flops 805437440 | bytes 2097157 | tf_op jit(solution)/shard_map/dot_general | solution.py:17
  62.6 1.0 convolution_convert_fusion
  63.6 12.0 %all_to_all.23 = bf16[4,128,256]{2,1,0:T(8,128)(2,1)} all-to-all(bf16[4,128,256]{2,1,0:T(8,128)(2,1)S(1)} %bitcast.23), channel_id=1, replica_groups=mesh['groups'=2,'shard'=4,'pair'=4] {'shard'}, dimensions={0} | all-to-all | bytes 524288 | tf_op jit(solution)/shard_map/all_to_all | solution.py:78
  75.6 0.0 all-gather.3.cloned.1.call-update
  75.6 16.0 %all-gather.3.cloned.1.call-done = bf16[16,128,256]{2,1,0:T(8,128)(2,1)} async-done(((bf16[4,128,256]{2,1,0:T(8,128)(2,1)}), bf16[16,128,256]{2,1,0:T(8,128)(2,1)}) %all-gather.3.cloned.1.call-update) | async-done | bytes 1048592 | tf_op jit(solution)/shard_map/all_gather | solution.py:80
  91.6 2.3 %copy.11 = bf16[1,2,4,128,2,256]{5,4,3,2,1,0:T(2,128)(2,1)S(1)} copy(bf16[1,2,4,128,2,256]{5,3,2,4,1,0:T(8,128)(2,1)} %bitcast.24) | data formatting | bytes 2097152 | tf_op jit(solution)/shard_map/transpose | solution.py:83
  93.9 1.5 %reshape.31 = bf16[1,8,128,512]{3,2,1,0:T(8,128)(2,1)} reshape(bf16[1,2,4,128,2,256]{5,4,3,2,1,0:T(2,128)(2,1)S(1)} %copy.11) | data formatting | bytes 2097152 | tf_op jit(solution)/shard_map/reshape | solution.py:84
  (5 shorter events, 0.0 us)
Async XLA Ops:
  9.1 20.8 %all-to-all-start = ((bf16[4,128,512]{2,1,0:T(8,128)(2,1)}), bf16[4,128,512]{2,1,0:T(8,128)(2,1)S(1)}, u32[]{:S(2)}, u32[]{:S(2)}) async-start(bf16[4,128,512]{2,1,0:T(8,128)(2,1)} %dynamic-slice_bitcast_fusion.1), calls=%async_computation | async-start | bytes 1048576 | tf_op jit(solution)/shard_map/all_to_all | solution.py:59
  37.6 2.1 %copy-start = (bf16[1,8,128,512]{3,2,1,0:T(8,128)(2,1)S(1)}, bf16[1,8,128,512]{3,2,1,0:T(8,128)(2,1)}, u32[]{:S(2)}) copy-start(bf16[1,8,128,512]{3,2,1,0:T(8,128)(2,1)} %param.2) | copy-start | bytes 3145732
  37.6 2.1 %copy-start.2 = (bf16[1,8,128,512]{3,2,1,0:T(8,128)(2,1)S(1)}, bf16[1,8,128,512]{3,2,1,0:T(8,128)(2,1)}, u32[]{:S(2)}) copy-start(bf16[1,8,128,512]{3,2,1,0:T(8,128)(2,1)} %param.3) | copy-start | bytes 3145732
  39.7 21.2 %collective-permute-start = (f32[512,512]{1,0:T(8,128)S(1)}, f32[512,512]{1,0:T(8,128)S(1)}, u32[]{:S(2)}, u32[]{:S(2)}) collective-permute-start(f32[512,512]{1,0:T(8,128)S(1)} %fusion.4), channel_id=1, source_target_pairs={{0,1},{1,0},{2,3},{3,2},{4,5},{5,4},{6,7},{7,6},{8,9},{9,8},{10,11... | collective-permute-start | bytes 3145736 | tf_op jit(solution)/shard_map/ppermute | solution.py:13
  40.1 1.1 %copy-start.1 = (bf16[1,8,128,512]{3,2,1,0:T(8,128)(2,1)}, bf16[1,8,128,512]{3,2,1,0:T(8,128)(2,1)S(1)}, u32[]{:S(2)}) copy-start(bf16[1,8,128,512]{3,2,1,0:T(8,128)(2,1)S(1)} %add_convert_fusion) | copy-start | bytes 3145732
  41.3 19.6 %all-to-all-start.1 = ((bf16[4,128,512]{2,1,0:T(8,128)(2,1)}), bf16[4,128,512]{2,1,0:T(8,128)(2,1)}, u32[]{:S(2)}, u32[]{:S(2)}) async-start(bf16[4,128,512]{2,1,0:T(8,128)(2,1)} %dynamic-slice_bitcast_fusion), calls=%async_computation.1 | async-start | bytes 1048576 | tf_op jit(solution)/shard_map/all_to_all | solution.py:60
  45.4 46.2 %all-gather.3.cloned.1.call-start = ((), (), s32[]{:S(2)}) async-start(), calls=%async_computation.3 | async-start | bytes 1310720 | tf_op jit(solution)/shard_map/all_gather | solution.py:80
Sparse Core Ops, SparseCore 0:
  75.7 15.7 all-gather.2
where the time goes:
time: 103 us; the launch traced here: 102 us
  waiting for transfers between devices  45.9 us (45%)
  between operations  14.9 us (14%)
  blocking collectives  12 us (12%)
  matrix products  11.5 us (11%)
  starting transfers between devices  10.6 us (10%)
  local copies, waits for them, and re-layouts  7.03 us (7%)
    all_gather x1, waiting for transfers between devices, local(): gathered = lax.all_gather(own_rows[None], 'pair', axis=0, tiled=True)  16 us
    all_to_all x1, waiting for transfers between devices, local(): lax.all_to_all(mom_half, 'shard', split_axis=0, concat_axis=1, tiled=True)  15.4 us
    all_to_all x1, waiting for transfers between devices, local(): lax.all_to_all(grad_half, 'shard', split_axis=0, concat_axis=1, tiled=True)  14.5 us
    all_to_all x1, blocking collectives, local(): lax.all_to_all(outgoing, 'shard', split_axis=0, concat_axis=0, tiled=True)  12 us
    dot_general x6, matrix products, multiply(): jnp.dot(left_matrix, right_matrix, precision=lax.Precision.HIGHEST, prefe...  10.4 us
    all_to_all x1, starting transfers between devices, local(): lax.all_to_all(grad_half, 'shard', split_axis=0, concat_axis=1, tiled=True)  6.35 us
    all_to_all x1, starting transfers between devices, local(): lax.all_to_all(mom_half, 'shard', split_axis=0, concat_axis=1, tiled=True)  4.14 us
    transpose x1, local copies, waits for them, and re-layouts, local(): update = gathered.reshape(2, 2, block_rows, half_cols, local_rows, half_w...  2.3 us
  transfers between devices with their start and end apart: 4, of which 3 were waited for; matrix products, arithmetic and copies ran while one was open for 1% of the time, Pallas kernels for 0%

commit v1 on v0

--- a/solution.py
+++ b/solution.py
@@ -77,7 +77,12 @@
     outgoing = own_piece.reshape(shards, local_rows, half_width)
     returned = lax.all_to_all(outgoing, "shard", split_axis=0, concat_axis=0, tiled=True)
     own_rows = returned.reshape(block_rows, half_cols, local_rows, half_width)
-    gathered = lax.all_gather(own_rows[None], "pair", axis=0, tiled=True)
+    ring = [own_rows[None]]
+    for hop in range(3):
+        ring.append(lax.ppermute(ring[-1], "pair", [(dev, (dev + 1) % 4) for dev in range(4)]))
+    gathered = jnp.roll(
+        jnp.concatenate(ring[::-1], axis=0), (lax.axis_index("pair") + 1) * ring[0].shape[0], axis=0
+    )
     update = (
         gathered.reshape(2, 2, block_rows, half_cols, local_rows, half_width)
         .transpose(2, 0, 3, 4, 1, 5)

time: 103 us -> 88.3 us (0.86)
  between operations: 14.9 us -> 1.59 us
  local copies, waits for them, and re-layouts: 7.03 us -> 5.24 us
  waiting for transfers between devices: 45.9 us -> 47.3 us
    ppermute x0 -> x3, waiting for transfers between devices: none -> 17.4 us  [local(): lax.ppermute(ring[-1], 'pair', [(dev, (dev + 1) % 4) for dev in range(4)])]
    all_gather x1 -> x0, waiting for transfers between devices: 16 us -> none  [local(): gathered = lax.all_gather(own_rows[None], 'pair', axis=0, tiled=True)]
    transpose x1, local copies, waits for them, and re-layouts: 2.3 us -> 0.66 us  [local(): update = gathered.reshape(2, 2, block_rows, half_cols, local_rows, half_w...]
    reshape x1 -> x0, local copies, waits for them, and re-layouts: 1.49 us -> none  [local(): update = gathered.reshape(2, 2, block_rows, half_cols, local_rows, half_w...]
    unnamed x6 -> x14, local copies, waits for them, and re-layouts: 0.26 us -> 1.47 us
  transfers between devices with their start and end apart: 4 -> 6, of which waited for: 3 -> 5; matrix products, arithmetic and copies ran while one was open for 1% -> 1% of each run, Pallas kernels for 0% -> 0%
where the time goes in v1:
time: 88.3 us; the launch traced here: 87.9 us
  waiting for transfers between devices  47.3 us (54%)
  matrix products  11.5 us (13%)
  blocking collectives  11.3 us (13%)
  starting transfers between devices  10.6 us (12%)
  local copies, waits for them, and re-layouts  5.24 us (6%)
  between operations  1.59 us (2%)
    ppermute x3, waiting for transfers between devices, local(): lax.ppermute(ring[-1], 'pair', [(dev, (dev + 1) % 4) for dev in range(4)])  17.4 us
    all_to_all x1, waiting for transfers between devices, local(): lax.all_to_all(mom_half, 'shard', split_axis=0, concat_axis=1, tiled=True)  15.5 us
    all_to_all x1, waiting for transfers between devices, local(): lax.all_to_all(grad_half, 'shard', split_axis=0, concat_axis=1, tiled=True)  14.5 us
    all_to_all x1, blocking collectives, local(): lax.all_to_all(outgoing, 'shard', split_axis=0, concat_axis=0, tiled=True)  11.3 us
    dot_general x6, matrix products, multiply(): jnp.dot(left_matrix, right_matrix, precision=lax.Precision.HIGHEST, prefe...  10.4 us
    all_to_all x1, starting transfers between devices, local(): lax.all_to_all(grad_half, 'shard', split_axis=0, concat_axis=1, tiled=True)  6.35 us
    all_to_all x1, starting transfers between devices, local(): lax.all_to_all(mom_half, 'shard', split_axis=0, concat_axis=1, tiled=True)  4.14 us
    reshape x1, local copies, waits for them, and re-layouts, local(): lax.dynamic_slice_in_dim(gradient, column_half * half_cols, half_cols, 1)  1.87 us
  transfers between devices with their start and end apart: 6, of which 5 were waited for; matrix products, arithmetic and copies ran while one was open for 1% of the time, Pallas kernels for 0%

profile of v1, /device:TPU:0, one launch (start us, length us, event | category | flops | bytes accessed | tf_op | source)
XLA Modules:
  0.0 87.9 jit_solution(2651183138997968309)
XLA Ops:
  0.6 1.9 %dynamic-slice_bitcast_fusion.1 = bf16[4,128,512]{2,1,0:T(8,128)(2,1)} fusion(bf16[1,8,128,512]{3,2,1,0:T(8,128)(2,1)} %param.2, s32[]{:T(128)S(6)} %select_n.56), kind=kLoop, calls=%fused_computation.23 | loop fusion | bytes 1048580 | tf_op jit(solution)/shard_map/reshape | solution.py:52
  2.5 6.3 %all-to-all-start = ((bf16[4,128,512]{2,1,0:T(8,128)(2,1)}), bf16[4,128,512]{2,1,0:T(8,128)(2,1)S(1)}, u32[]{:S(2)}, u32[]{:S(2)}) async-start(bf16[4,128,512]{2,1,0:T(8,128)(2,1)} %dynamic-slice_bitcast_fusion.1), calls=%async_computation | async-start | bytes 1048576 | tf_op jit(solution)/shard_map/all_to_all | solution.py:59
  8.9 14.5 %all-to-all-done = bf16[4,128,512]{2,1,0:T(8,128)(2,1)S(1)} async-done(((bf16[4,128,512]{2,1,0:T(8,128)(2,1)}), bf16[4,128,512]{2,1,0:T(8,128)(2,1)S(1)}, u32[]{:S(2)}, u32[]{:S(2)}) %all-to-all-start) | async-done | bytes 524320 | tf_op jit(solution)/shard_map/all_to_all | solution.py:59
  23.4 0.2 copy.11
  23.6 1.1 %select_reduce_fusion = (f32[]{:T(128)}, f32[512,512]{1,0:T(8,128)S(1)}) fusion(bf16[512,512]{1,0:T(8,128)(2,1)S(1)} %bitcast.29, bf16[512,512]{0,1:T(8,128)(2,1)S(1)} %copy.11, pred[]{:T(512)S(6)} %eq.20), kind=kOutput, calls=%fused_computation.11 | convolution fusion | flops 270270464 | bytes 2097157 | tf_op jit(solution)/shard_map/dot_general | solution.py:67
  25.4 2.0 %fusion.6 = f32[512,512]{1,0:T(8,128)S(1)} fusion(f32[512,512]{1,0:T(8,128)S(1)} %get-tuple-element.5, f32[]{:T(128)S(6)} %div.40), kind=kOutput, calls=%fused_computation.13 | convolution fusion | flops 1611923456 | bytes 2097156 | tf_op jit(solution)/shard_map/dot_general | solution.py:17
  27.4 1.8 %fusion.28 = f32[512,512]{1,0:T(8,128)S(1)} fusion(f32[512,512]{1,0:T(8,128)S(1)} %fusion.6), kind=kOutput, calls=%fused_computation.47 | convolution fusion | flops 1610612736 | bytes 2097152 | tf_op jit(solution)/shard_map/dot_general | solution.py:17
  29.2 1.9 %fusion.1 = f32[512,512]{1,0:T(8,128)S(1)} fusion(f32[512,512]{1,0:T(8,128)S(1)} %fusion.28, f32[512,512]{1,0:T(8,128)S(1)} %get-tuple-element.5, f32[]{:T(128)S(6)} %div.40), kind=kOutput, calls=%fused_computation.5 | convolution fusion | flops 1611923456 | bytes 3145732 | tf_op jit(solution)/shard_map/dot_general | solution.py:17
  31.1 0.0 copy-start
  31.1 2.0 %fusion.4 = f32[512,512]{1,0:T(8,128)S(1)} fusion(f32[512,512]{1,0:T(8,128)S(1)} %fusion.1, f32[]{:T(128)S(6)} %sqrt.7, f32[512,512]{1,0:T(8,128)S(1)} %get-tuple-element.5, f32[]{:T(128)S(6)} %div.40), kind=kOutput, calls=%fused_computation.9 | convolution fusion | flops 1612185600 | bytes 3145736 | tf_op jit(solution)/shard_map/dot_general | solution.py:17
  33.1 0.1 collective-permute-start
  33.2 0.4 add_convert_fusion
  33.6 0.9 %dynamic-slice_bitcast_fusion = bf16[4,128,512]{2,1,0:T(8,128)(2,1)} fusion(bf16[1,8,128,512]{3,2,1,0:T(8,128)(2,1)S(1)} %add_convert_fusion, s32[]{:T(128)S(6)} %select_n.56), kind=kLoop, calls=%fused_computation.18 | loop fusion | bytes 1048580 | tf_op jit(solution)/shard_map/reshape | solution.py:57
  34.5 4.1 %all-to-all-start.1 = ((bf16[4,128,512]{2,1,0:T(8,128)(2,1)}), bf16[4,128,512]{2,1,0:T(8,128)(2,1)}, u32[]{:S(2)}, u32[]{:S(2)}) async-start(bf16[4,128,512]{2,1,0:T(8,128)(2,1)} %dynamic-slice_bitcast_fusion), calls=%async_computation.1 | async-start | bytes 1048576 | tf_op jit(solution)/shard_map/all_to_all | solution.py:60
  38.7 15.5 %all-to-all-done.1 = bf16[4,128,512]{2,1,0:T(8,128)(2,1)} async-done(((bf16[4,128,512]{2,1,0:T(8,128)(2,1)}), bf16[4,128,512]{2,1,0:T(8,128)(2,1)}, u32[]{:S(2)}, u32[]{:S(2)}) %all-to-all-start.1) | async-done | bytes 524320 | tf_op jit(solution)/shard_map/all_to_all | solution.py:60
  54.1 1.7 %fusion.9 = f32[512,256]{1,0:T(8,128)S(1)} fusion(bf16[512,512]{1,0:T(8,128)(2,1)} %bitcast.4, f32[512,512]{1,0:T(8,128)S(1)} %fusion.4, s32[]{:T(128)S(6)} %select_n.61, f32[512,512]{1,0:T(8,128)S(1)} %collective-permute-done, pred[]{:T(512)S(6)} %eq.20), kind=kOutput, calls=%fused_computation.15 | convolution fusion | flops 805437440 | bytes 2097157 | tf_op jit(solution)/shard_map/dot_general | solution.py:17
  55.9 1.0 %convolution_convert_fusion = bf16[512,256]{1,0:T(8,128)(2,1)S(1)} fusion(f32[512,256]{1,0:T(8,128)S(1)} %fusion.9, f32[512,512]{1,0:T(8,128)S(1)} %fusion.4, f32[512,512]{1,0:T(8,128)S(1)} %collective-permute-done, pred[]{:T(512)S(6)} %eq.20), kind=kOutput, calls=%fused_computation.6 | convolution fusion | flops 805699584 | bytes 2883585 | tf_op jit(solution)/shard_map/dot_general | solution.py:17
  56.9 11.3 %all_to_all.23 = bf16[4,128,256]{2,1,0:T(8,128)(2,1)S(1)} all-to-all(bf16[4,128,256]{2,1,0:T(8,128)(2,1)S(1)} %bitcast.30), channel_id=1, replica_groups=mesh['groups'=2,'shard'=4,'pair'=4] {'shard'}, dimensions={0} | all-to-all | bytes 524288 | tf_op jit(solution)/shard_map/all_to_all | solution.py:78
  68.2 5.8 %collective-permute-done.1 = bf16[1,1,4,128,256]{4,3,2,0,1:T(8,128)(2,1)S(1)} collective-permute-done((bf16[1,1,4,128,256]{4,3,2,0,1:T(8,128)(2,1)S(1)}, bf16[1,1,4,128,256]{4,3,2,0,1:T(8,128)(2,1)S(1)}, u32[]{:S(2)}, u32[]{:S(2)}) %collective-permute-start.1) | collective-permute-done | bytes 262176 | tf_op jit(solution)/shard_map/ppermute | solution.py:82
  74.0 5.8 %collective-permute-done.2 = bf16[1,1,4,128,256]{4,3,2,0,1:T(8,128)(2,1)S(1)} collective-permute-done((bf16[1,1,4,128,256]{4,3,2,0,1:T(8,128)(2,1)S(1)}, bf16[1,1,4,128,256]{4,3,2,0,1:T(8,128)(2,1)S(1)}, u32[]{:S(2)}, u32[]{:S(2)}) %collective-permute-start.2) | collective-permute-done | bytes 262176 | tf_op jit(solution)/shard_map/ppermute | solution.py:82
  79.8 5.8 %collective-permute-done.3 = bf16[1,1,4,128,256]{4,3,2,0,1:T(8,128)(2,1)S(1)} collective-permute-done((bf16[1,1,4,128,256]{4,3,2,0,1:T(8,128)(2,1)S(1)}, bf16[1,1,4,128,256]{4,3,2,0,1:T(8,128)(2,1)S(1)}, u32[]{:S(2)}, u32[]{:S(2)}) %collective-permute-start.3) | collective-permute-done | bytes 262176 | tf_op jit(solution)/shard_map/ppermute | solution.py:82
  85.8 0.1 constant_dynamic-slice_fusion
  85.9 0.7 copy.9
  86.6 1.3 %copy.10 = bf16[1,8,128,512]{3,2,1,0:T(8,128)(2,1)} copy(bf16[1,8,128,512]{2,3,1,0:T(8,128)(2,1)S(1)} %bitcast.26) | data formatting | bytes 2097152
  (17 shorter events, 0.2 us)
Async XLA Ops:
  2.5 20.8 %all-to-all-start = ((bf16[4,128,512]{2,1,0:T(8,128)(2,1)}), bf16[4,128,512]{2,1,0:T(8,128)(2,1)S(1)}, u32[]{:S(2)}, u32[]{:S(2)}) async-start(bf16[4,128,512]{2,1,0:T(8,128)(2,1)} %dynamic-slice_bitcast_fusion.1), calls=%async_computation | async-start | bytes 1048576 | tf_op jit(solution)/shard_map/all_to_all | solution.py:59
  31.1 2.1 %copy-start = (bf16[1,8,128,512]{3,2,1,0:T(8,128)(2,1)S(1)}, bf16[1,8,128,512]{3,2,1,0:T(8,128)(2,1)}, u32[]{:S(2)}) copy-start(bf16[1,8,128,512]{3,2,1,0:T(8,128)(2,1)} %param.2) | copy-start | bytes 3145732
  31.1 2.1 %copy-start.2 = (bf16[1,8,128,512]{3,2,1,0:T(8,128)(2,1)S(1)}, bf16[1,8,128,512]{3,2,1,0:T(8,128)(2,1)}, u32[]{:S(2)}) copy-start(bf16[1,8,128,512]{3,2,1,0:T(8,128)(2,1)} %param.3) | copy-start | bytes 3145732
  33.1 21.0 %collective-permute-start = (f32[512,512]{1,0:T(8,128)S(1)}, f32[512,512]{1,0:T(8,128)S(1)}, u32[]{:S(2)}, u32[]{:S(2)}) collective-permute-start(f32[512,512]{1,0:T(8,128)S(1)} %fusion.4), channel_id=1, source_target_pairs={{0,1},{1,0},{2,3},{3,2},{4,5},{5,4},{6,7},{7,6},{8,9},{9,8},{10,11... | collective-permute-start | bytes 3145736 | tf_op jit(solution)/shard_map/ppermute | solution.py:13
  33.6 22.3 %copy-start.1 = (bf16[1,8,128,512]{3,2,1,0:T(8,128)(2,1)}, bf16[1,8,128,512]{3,2,1,0:T(8,128)(2,1)S(1)}, u32[]{:S(2)}) copy-start(bf16[1,8,128,512]{3,2,1,0:T(8,128)(2,1)S(1)} %add_convert_fusion) | copy-start | bytes 3145732
  34.5 19.6 %all-to-all-start.1 = ((bf16[4,128,512]{2,1,0:T(8,128)(2,1)}), bf16[4,128,512]{2,1,0:T(8,128)(2,1)}, u32[]{:S(2)}, u32[]{:S(2)}) async-start(bf16[4,128,512]{2,1,0:T(8,128)(2,1)} %dynamic-slice_bitcast_fusion), calls=%async_computation.1 | async-start | bytes 1048576 | tf_op jit(solution)/shard_map/all_to_all | solution.py:60
  68.2 5.8 %collective-permute-start.1 = (bf16[1,1,4,128,256]{4,3,2,0,1:T(8,128)(2,1)S(1)}, bf16[1,1,4,128,256]{4,3,2,0,1:T(8,128)(2,1)S(1)}, u32[]{:S(2)}, u32[]{:S(2)}) collective-permute-start(bf16[1,1,4,128,256]{4,3,2,0,1:T(8,128)(2,1)S(1)} %bitcast.27), channel_id=1, source_target_pairs={{0,1},{1,2},{2,3},{3,0},{4,5},{5,6},{6,7},{7,4},{8,9},{9,10},{10,1... | collective-permute-start | bytes 786440 | tf_op jit(solution)/shard_map/ppermute | solution.py:82
  74.0 5.8 %collective-permute-start.2 = (bf16[1,1,4,128,256]{4,3,2,0,1:T(8,128)(2,1)S(1)}, bf16[1,1,4,128,256]{4,3,2,0,1:T(8,128)(2,1)S(1)}, u32[]{:S(2)}, u32[]{:S(2)}) collective-permute-start(bf16[1,1,4,128,256]{4,3,2,0,1:T(8,128)(2,1)S(1)} %collective-permute-done.1), channel_id=1, source_target_pairs={{0,1},{1,2},{2,3},{3,0},{4,5},{5,6},{6,7},{7,4},{8,9},{9,10},{10,1... | collective-permute-start | bytes 786440 | tf_op jit(solution)/shard_map/ppermute | solution.py:82
  79.8 5.8 %collective-permute-start.3 = (bf16[1,1,4,128,256]{4,3,2,0,1:T(8,128)(2,1)S(1)}, bf16[1,1,4,128,256]{4,3,2,0,1:T(8,128)(2,1)S(1)}, u32[]{:S(2)}, u32[]{:S(2)}) collective-permute-start(bf16[1,1,4,128,256]{4,3,2,0,1:T(8,128)(2,1)S(1)} %collective-permute-done.2), channel_id=1, source_target_pairs={{0,1},{1,2},{2,3},{3,0},{4,5},{5,6},{6,7},{7,4},{8,9},{9,10},{10,1... | collective-permute-start | bytes 786440 | tf_op jit(solution)/shard_map/ppermute | solution.py:82
